TPU v7x, 32 devices: a whole 2x2x4 slice. The times are simulated.
32 devices in a mesh: dp: 2 (over x), row: 4 (over z), col: 4 (over y, core).
Axes of the slice: x: 2, y: 2, z: 4, core: 2. Of those that a mesh axis runs over, the one named last changes fastest.
Arguments:
- features: bfloat16 [2, 128, 128, 320], P('dp', 'row', 'col'), may hold values from -20 to 20
- norm1_gain: float32 [320], replicated, may hold values from 0.1 to 1.9
- conv1_kernel: bfloat16 [320, 9, 320], P('dp'), may hold values from -0.109375 to 0.109375
- norm2_gain: float32 [320], replicated, may hold values from 0.1 to 1.9
- conv2_kernel: bfloat16 [320, 9, 320], P('dp'), may hold values from -0.109375 to 0.109375
Outputs:
- block_out: bfloat16 [2, 128, 128, 320], P('dp', 'row', 'col')
All inputs are finite; a program needn't handle non-finite values.
Results may differ from a plain program's by a relative error of at most 0.007.
Values may be sent and summed in bfloat16 or wider, within the bound.
No kernel may reach another device: no remote copies, remote signals or barrier semaphores. Data moves between devices by JAX's collectives and lax.ppermute only.
A program may use at most 64 MiB of HBM per device.

v0:
```python
import jax
import jax.numpy as jnp
from jax import lax
from jax.sharding import PartitionSpec as P

GROUPS = 32
EPS = 1e-05


def extended(value, sides, width):
    for axis, dim in sides:
        size, length = (lax.axis_size(axis), value.shape[dim])
        up = [(i, (i + 1) % size) for i in range(size - 1)]
        down = [(j, i) for i, j in up]
        last = lax.slice_in_dim(value, length - width, length, axis=dim)
        initial = lax.slice_in_dim(value, 0, width, axis=dim)
        before = lax.ppermute(last, axis, up)
        after = lax.ppermute(initial, axis, down)
        value = jnp.concatenate([before, value, after], axis=dim)
    return value


def normalize(values, scale_gain, count):
    batch_dev, tile_rows, tile_cols, width = values.shape
    grouped = values.astype(jnp.float32).reshape(
        batch_dev, tile_rows * tile_cols, GROUPS, width // GROUPS
    )
    totals, squares = lax.psum(
        (jnp.sum(grouped, axis=(1, 3)), jnp.sum(grouped * grouped, axis=(1, 3))), ("row", "col")
    )
    average_flat = totals / count
    spread = squares / count - average_flat * average_flat
    centred = grouped - average_flat[:, None, :, None]
    scaled = centred * lax.rsqrt(spread + EPS)[:, None, :, None]
    normed = scaled.reshape(values.shape) * scale_gain
    return jax.nn.silu(normed).astype(jnp.bfloat16)


def tap_stack(values):
    padded = extended(values, (("row", 1), ("col", 2)), 1)
    tile_rows, tile_cols, width = (values.shape[1], values.shape[2], values.shape[3])
    pieces = [
        padded[:, shift_row : shift_row + tile_rows, shift_col : shift_col + tile_cols, :]
        for shift_row in range(3)
        for shift_col in range(3)
    ]
    return jnp.concatenate(pieces, axis=-1).reshape(-1, 9 * width)


def finish(stacked, whole_kernel, skip_flat):
    flat_kernel = whole_kernel.reshape(whole_kernel.shape[0], -1)
    result = lax.dot_general(
        stacked, flat_kernel, (((1,), (1,)), ((), ())), preferred_element_type=jnp.float32
    )
    if skip_flat is not None:
        result = result + skip_flat.astype(jnp.float32)
    return result.astype(jnp.bfloat16)


def convolve_gathered(stacked, kernel, skip_flat):
    whole_kernel = lax.all_gather(kernel, "dp", axis=0, tiled=True)
    return finish(stacked, whole_kernel, skip_flat)


def local(features, norm1_gain, conv1_kernel, norm2_gain, conv2_kernel):
    batch_dev, tile_rows, tile_cols, width = features.shape
    count = tile_rows * tile_cols * lax.axis_size("row") * lax.axis_size("col") * (width // GROUPS)
    first_act = normalize(features, norm1_gain, count)
    first_stack = tap_stack(first_act)
    middle = convolve_gathered(first_stack, conv1_kernel, None)
    middle = middle.reshape(batch_dev, tile_rows, tile_cols, width)
    second_act = normalize(middle, norm2_gain, count)
    second_stack = tap_stack(second_act)
    skip_flat = features.reshape(-1, width)
    block_out = convolve_gathered(second_stack, conv2_kernel, skip_flat)
    return block_out.reshape(batch_dev, tile_rows, tile_cols, width)


def solution(mesh):
    return jax.shard_map(
        local,
        mesh=mesh,
        in_specs=(P("dp", "row", "col", None), P(), P("dp", None, None), P(), P("dp", None, None)),
        out_specs=P("dp", "row", "col", None),
        check_vma=False,
    )
```

profile of v0, /device:TPU:9, one launch (start us, length us, event | category | flops | bytes accessed | tf_op | source)
XLA Modules:
  0.0 162.9 jit_solution(10472760439591955007)
XLA Ops:
  7.3 1.4 convert_reduce_fusion
  9.2 22.4 %all-reduce.1 = (f32[1,32]{1,0:T(1,128)S(1)}, f32[1,32]{1,0:T(1,128)S(1)}) all-reduce(f32[1,32]{1,0:T(1,128)S(1)} %bitcast.63, f32[1,32]{1,0:T(1,128)S(1)} %bitcast.61), channel_id=1, replica_groups=mesh['dp'=2,'row'=4,'col'=4] {'row','col'}, use_global_device_ids=true, to_apply=%region_5.6 | all-reduce | flops 64 | bytes 512 | tf_op jit(solution)/shard_map/psum | solution.py:28
  33.2 3.2 %collective-permute-start = (bf16[1,1,32,320]{3,2,1,0:T(8,128)(2,1)S(1)}, bf16[1,1,32,320]{3,2,1,0:T(8,128)(2,1)S(1)}, u32[]{:S(2)}, u32[]{:S(2)}) collective-permute-start(bf16[1,1,32,320]{3,2,1,0:T(8,128)(2,1)S(1)} %get-tuple-element.39), channel_id=1, source_target_pairs={{0,4},{4,8},{8,12},{1,5},{5,9},{9,13},{2,6},{6,10},{10,14},{3,7},{... | collective-permute-start | bytes 61448 | tf_op jit(solution)/shard_map/ppermute | solution.py:17
  36.4 7.5 %collective-permute-start.1 = (bf16[1,1,32,320]{3,2,1,0:T(8,128)(2,1)S(1)}, bf16[1,1,32,320]{3,2,1,0:T(8,128)(2,1)S(1)}, u32[]{:S(2)}, u32[]{:S(2)}) collective-permute-start(bf16[1,1,32,320]{3,2,1,0:T(8,128)(2,1)S(1)} %get-tuple-element.40), channel_id=1, source_target_pairs={{4,0},{8,4},{12,8},{5,1},{9,5},{13,9},{6,2},{10,6},{14,10},{7,3},{... | collective-permute-start | bytes 61448 | tf_op jit(solution)/shard_map/ppermute | solution.py:18
  44.9 4.8 %collective-permute-start.2 = (bf16[1,34,1,320]{3,2,1,0:T(2,128)(2,1)S(1)}, bf16[1,34,1,320]{3,2,1,0:T(2,128)(2,1)S(1)}, u32[]{:S(2)}, u32[]{:S(2)}) collective-permute-start(bf16[1,34,1,320]{3,2,1,0:T(2,128)(2,1)S(1)} %get-tuple-element.32), channel_id=1, source_target_pairs={{0,1},{1,2},{2,3},{4,5},{5,6},{6,7},{8,9},{9,10},{10,11},{12,13},{... | collective-permute-start | bytes 65288 | tf_op jit(solution)/shard_map/ppermute | solution.py:17
  49.7 3.6 %collective-permute-start.3 = (bf16[1,34,1,320]{3,2,1,0:T(2,128)(2,1)S(1)}, bf16[1,34,1,320]{3,2,1,0:T(2,128)(2,1)S(1)}, u32[]{:S(2)}, u32[]{:S(2)}) collective-permute-start(bf16[1,34,1,320]{3,2,1,0:T(2,128)(2,1)S(1)} %get-tuple-element.31), channel_id=1, source_target_pairs={{1,0},{2,1},{3,2},{5,4},{6,5},{7,6},{9,8},{10,9},{11,10},{13,12},{... | collective-permute-start | bytes 65288 | tf_op jit(solution)/shard_map/ppermute | solution.py:18
  55.8 1.9 %fusion.6 = (bf16[1,32,32,320]{3,2,1,0:T(8,128)(2,1)S(1)}, bf16[1,32,32,320]{3,2,1,0:T(8,128)(2,1)S(1)}, bf16[1,32,32,320]{3,2,1,0:T(8,128)(2,1)}, bf16[1,32,32,...) fusion(bf16[1,34,33,320]{3,2,1,0:T(8,128)(2,1)S(1)} %get-tuple-element.29, ...), kind=kLoop, calls=%fused_computation.40 | loop fusion | bytes 7864320 | tf_op jit(solution)/shard_map/slice | solution.py:43
  57.7 10.1 %concatenate.96 = bf16[1024,2880]{1,0:T(8,128)(2,1)} concatenate(bf16[1024,320]{1,0:T(8,128)(2,1)} %bitcast.45, bf16[1024,320]{1,0:T(8,128)(2,1)} %bitcast.50, bf16[1024,320]{1,0:T(8,128)(2,1)} %bitcast.44, bf16[1024,320]{1,0:T(8,128)(2,1)} %bitcast.46, bf16[1024,320]{1,0:T(8,128)(2,1)S(1)} %bitcast.39, bf16[1024,320]{1,0:T(8,128)(2,1)S(1)} %bitcast.43, ...), dimensions={1} | concatenate | bytes 11796480 | tf_op jit(solution)/shard_map/concatenate | solution.py:47
  67.8 4.2 %copy.17 = bf16[320,9,320]{0,2,1:T(8,128)(2,1)} copy(bf16[320,9,320]{2,0,1:T(8,128)(2,1)} %all-gather.3.cloned.1.call-done) | data formatting | bytes 3686400 | tf_op jit(solution)/shard_map/all_gather | solution.py:61
  72.0 6.7 %fusion.3 = (f32[320]{0:T(512)S(1)}, f32[320]{0:T(512)S(1)}, f32[1024,320]{0,1:T(8,128)}) fusion(bf16[1024,2880]{1,0:T(8,128)(2,1)} %concatenate.96, bf16[320,2880]{0,1:T(8,128)(2,1)} %bitcast.59), kind=kOutput, calls=%fused_computation.37 | convolution fusion | flops 1889074688 | bytes 9054720 | tf_op jit(solution)/shard_map/dot_general | solution.py:52
  79.2 22.1 %all-reduce = (f32[1,32]{1,0:T(1,128)S(1)}, f32[1,32]{1,0:T(1,128)S(1)}) all-reduce(f32[1,32]{1,0:T(1,128)S(1)} %bitcast.62, f32[1,32]{1,0:T(1,128)S(1)} %bitcast.60), channel_id=1, replica_groups=mesh['dp'=2,'row'=4,'col'=4] {'row','col'}, use_global_device_ids=true, to_apply=%region_11.12 | all-reduce | flops 64 | bytes 512 | tf_op jit(solution)/shard_map/psum | solution.py:28
  101.7 1.8 %copy.18 = f32[1024,320]{1,0:T(8,128)S(1)} copy(f32[1024,320]{0,1:T(8,128)} %get-tuple-element.45) | data formatting | bytes 2621440 | tf_op jit(solution)/shard_map/convert_element_type | solution.py:25
  104.0 1.9 %collective-permute-start.4 = (bf16[1,1,32,320]{3,2,1,0:T(8,128)(2,1)S(1)}, bf16[1,1,32,320]{3,2,1,0:T(8,128)(2,1)S(1)}, u32[]{:S(2)}, u32[]{:S(2)}) collective-permute-start(bf16[1,1,32,320]{3,2,1,0:T(8,128)(2,1)S(1)} %get-tuple-element.35), channel_id=1, source_target_pairs={{0,4},{4,8},{8,12},{1,5},{5,9},{9,13},{2,6},{6,10},{10,14},{3,7},{... | collective-permute-start | bytes 61448 | tf_op jit(solution)/shard_map/ppermute | solution.py:17
  105.9 9.5 %collective-permute-start.5 = (bf16[1,1,32,320]{3,2,1,0:T(8,128)(2,1)S(1)}, bf16[1,1,32,320]{3,2,1,0:T(8,128)(2,1)S(1)}, u32[]{:S(2)}, u32[]{:S(2)}) collective-permute-start(bf16[1,1,32,320]{3,2,1,0:T(8,128)(2,1)S(1)} %get-tuple-element.36), channel_id=1, source_target_pairs={{4,0},{8,4},{12,8},{5,1},{9,5},{13,9},{6,2},{10,6},{14,10},{7,3},{... | collective-permute-start | bytes 61448 | tf_op jit(solution)/shard_map/ppermute | solution.py:18
  116.7 4.2 %copy.27 = bf16[320,9,320]{0,2,1:T(8,128)(2,1)} copy(bf16[320,9,320]{2,0,1:T(8,128)(2,1)} %all-gather.5.cloned.1.call-done) | data formatting | bytes 3686400 | tf_op jit(solution)/shard_map/all_gather | solution.py:61
  121.1 1.9 %collective-permute-start.6 = (bf16[1,34,1,320]{3,2,1,0:T(2,128)(2,1)S(1)}, bf16[1,34,1,320]{3,2,1,0:T(2,128)(2,1)S(1)}, u32[]{:S(2)}, u32[]{:S(2)}) collective-permute-start(bf16[1,34,1,320]{3,2,1,0:T(2,128)(2,1)S(1)} %get-tuple-element.28), channel_id=1, source_target_pairs={{0,1},{1,2},{2,3},{4,5},{5,6},{6,7},{8,9},{9,10},{10,11},{12,13},{... | collective-permute-start | bytes 65288 | tf_op jit(solution)/shard_map/ppermute | solution.py:17
  123.0 3.1 %collective-permute-start.7 = (bf16[1,34,1,320]{3,2,1,0:T(2,128)(2,1)S(1)}, bf16[1,34,1,320]{3,2,1,0:T(2,128)(2,1)S(1)}, u32[]{:S(2)}, u32[]{:S(2)}) collective-permute-start(bf16[1,34,1,320]{3,2,1,0:T(2,128)(2,1)S(1)} %get-tuple-element.27), channel_id=1, source_target_pairs={{1,0},{2,1},{3,2},{5,4},{6,5},{7,6},{9,8},{10,9},{11,10},{13,12},{... | collective-permute-start | bytes 65288 | tf_op jit(solution)/shard_map/ppermute | solution.py:18
  130.5 2.0 %constant_dynamic-update-slice_fusion.7 = bf16[1024,2880]{0,1:T(8,128)(2,1)} fusion(bf16[1024,320]{0,1:T(8,128)(2,1)} %copy.19), kind=kLoop, calls=%fused_computation.32 | loop fusion | bytes 1310720
  132.5 1.5 fusion.4
  137.2 2.0 %constant_dynamic-update-slice_fusion.5 = bf16[1024,2880]{0,1:T(8,128)(2,1)} fusion(bf16[1024,2880]{0,1:T(8,128)(2,1)} %constant_dynamic-update-slice_fusion.6, bf16[1024,320]{0,1:T(8,128)(2,1)} %copy.21), kind=kLoop, calls=%fused_computation.30 | loop fusion | bytes 1310720
  140.1 1.4 fusion.2
  141.5 2.2 %copy.23 = bf16[1024,320]{0,1:T(8,128)(2,1)} copy(bf16[1024,320]{1,0:T(8,128)(2,1)} %bitcast.52) | data formatting | bytes 1310720 | tf_op jit(solution)/shard_map/concatenate | solution.py:47
  145.2 2.1 %constant_dynamic-update-slice_fusion.3 = bf16[1024,2880]{0,1:T(8,128)(2,1)} fusion(bf16[1024,2880]{0,1:T(8,128)(2,1)} %fusion.2, bf16[1024,320]{0,1:T(8,128)(2,1)} %copy.23), kind=kLoop, calls=%fused_computation.28 | loop fusion | bytes 1310720
  150.0 4.9 %fusion = bf16[1024,320]{0,1:T(8,128)(2,1)S(1)} fusion(f32[1024,320]{0,1:T(8,128)S(1)} %copy-done.8, bf16[1024,2880]{0,1:T(8,128)(2,1)} %constant_dynamic-update-slice_fusion, bf16[320,2880]{0,1:T(8,128)(2,1)S(1)} %bitcast.58), kind=kOutput, calls=%fused_computation.4 | convolution fusion | flops 1888092160 | bytes 9707520 | tf_op jit(solution)/shard_map/dot_general | solution.py:52
  (77 shorter events, 22.7 us)
Async XLA Ops:
  6.5 25.4 %copy-start = (bf16[1,32,32,320]{3,2,1,0:T(8,128)(2,1)S(1)}, bf16[1,32,32,320]{3,2,1,0:T(8,128)(2,1)}, u32[]{:S(2)}) copy-start(bf16[1,32,32,320]{3,2,1,0:T(8,128)(2,1)} %param.5) | copy-start | bytes 1966084
  6.5 61.3 %all-gather.3.cloned.1.call-start = ((), (), s32[]{:S(2)}) async-start(), calls=%async_computation | async-start | bytes 3317760 | tf_op jit(solution)/shard_map/all_gather | solution.py:61
  7.3 109.5 %all-gather.5.cloned.1.call-start = ((), (), s32[]{:S(2)}) async-start(), calls=%async_computation.1 | async-start | bytes 3317760 | tf_op jit(solution)/shard_map/all_gather | solution.py:61
  33.2 10.7 %collective-permute-start = (bf16[1,1,32,320]{3,2,1,0:T(8,128)(2,1)S(1)}, bf16[1,1,32,320]{3,2,1,0:T(8,128)(2,1)S(1)}, u32[]{:S(2)}, u32[]{:S(2)}) collective-permute-start(bf16[1,1,32,320]{3,2,1,0:T(8,128)(2,1)S(1)} %get-tuple-element.39), channel_id=1, source_target_pairs={{0,4},{4,8},{8,12},{1,5},{5,9},{9,13},{2,6},{6,10},{10,14},{3,7},{... | collective-permute-start | bytes 61448 | tf_op jit(solution)/shard_map/ppermute | solution.py:17
  36.4 8.4 %collective-permute-start.1 = (bf16[1,1,32,320]{3,2,1,0:T(8,128)(2,1)S(1)}, bf16[1,1,32,320]{3,2,1,0:T(8,128)(2,1)S(1)}, u32[]{:S(2)}, u32[]{:S(2)}) collective-permute-start(bf16[1,1,32,320]{3,2,1,0:T(8,128)(2,1)S(1)} %get-tuple-element.40), channel_id=1, source_target_pairs={{4,0},{8,4},{12,8},{5,1},{9,5},{13,9},{6,2},{10,6},{14,10},{7,3},{... | collective-permute-start | bytes 61448 | tf_op jit(solution)/shard_map/ppermute | solution.py:18
  44.9 9.9 %collective-permute-start.2 = (bf16[1,34,1,320]{3,2,1,0:T(2,128)(2,1)S(1)}, bf16[1,34,1,320]{3,2,1,0:T(2,128)(2,1)S(1)}, u32[]{:S(2)}, u32[]{:S(2)}) collective-permute-start(bf16[1,34,1,320]{3,2,1,0:T(2,128)(2,1)S(1)} %get-tuple-element.32), channel_id=1, source_target_pairs={{0,1},{1,2},{2,3},{4,5},{5,6},{6,7},{8,9},{9,10},{10,11},{12,13},{... | collective-permute-start | bytes 65288 | tf_op jit(solution)/shard_map/ppermute | solution.py:17
  49.7 5.4 %collective-permute-start.3 = (bf16[1,34,1,320]{3,2,1,0:T(2,128)(2,1)S(1)}, bf16[1,34,1,320]{3,2,1,0:T(2,128)(2,1)S(1)}, u32[]{:S(2)}, u32[]{:S(2)}) collective-permute-start(bf16[1,34,1,320]{3,2,1,0:T(2,128)(2,1)S(1)} %get-tuple-element.31), channel_id=1, source_target_pairs={{1,0},{2,1},{3,2},{5,4},{6,5},{7,6},{9,8},{10,9},{11,10},{13,12},{... | collective-permute-start | bytes 65288 | tf_op jit(solution)/shard_map/ppermute | solution.py:18
  78.7 24.7 %copy-start.9 = (f32[320]{0:T(512)S(1)}, f32[320]{0:T(512)}, u32[]{:S(2)}) copy-start(f32[320]{0:T(512)} %param.8) | copy-start | bytes 3844
  104.0 17.0 %collective-permute-start.4 = (bf16[1,1,32,320]{3,2,1,0:T(8,128)(2,1)S(1)}, bf16[1,1,32,320]{3,2,1,0:T(8,128)(2,1)S(1)}, u32[]{:S(2)}, u32[]{:S(2)}) collective-permute-start(bf16[1,1,32,320]{3,2,1,0:T(8,128)(2,1)S(1)} %get-tuple-element.35), channel_id=1, source_target_pairs={{0,4},{4,8},{8,12},{1,5},{5,9},{9,13},{2,6},{6,10},{10,14},{3,7},{... | collective-permute-start | bytes 61448 | tf_op jit(solution)/shard_map/ppermute | solution.py:17
  105.9 15.0 %collective-permute-start.5 = (bf16[1,1,32,320]{3,2,1,0:T(8,128)(2,1)S(1)}, bf16[1,1,32,320]{3,2,1,0:T(8,128)(2,1)S(1)}, u32[]{:S(2)}, u32[]{:S(2)}) collective-permute-start(bf16[1,1,32,320]{3,2,1,0:T(8,128)(2,1)S(1)} %get-tuple-element.36), channel_id=1, source_target_pairs={{4,0},{8,4},{12,8},{5,1},{9,5},{13,9},{6,2},{10,6},{14,10},{7,3},{... | collective-permute-start | bytes 61448 | tf_op jit(solution)/shard_map/ppermute | solution.py:18
  121.1 7.5 %collective-permute-start.6 = (bf16[1,34,1,320]{3,2,1,0:T(2,128)(2,1)S(1)}, bf16[1,34,1,320]{3,2,1,0:T(2,128)(2,1)S(1)}, u32[]{:S(2)}, u32[]{:S(2)}) collective-permute-start(bf16[1,34,1,320]{3,2,1,0:T(2,128)(2,1)S(1)} %get-tuple-element.28), channel_id=1, source_target_pairs={{0,1},{1,2},{2,3},{4,5},{5,6},{6,7},{8,9},{9,10},{10,11},{12,13},{... | collective-permute-start | bytes 65288 | tf_op jit(solution)/shard_map/ppermute | solution.py:17
  123.0 5.6 %collective-permute-start.7 = (bf16[1,34,1,320]{3,2,1,0:T(2,128)(2,1)S(1)}, bf16[1,34,1,320]{3,2,1,0:T(2,128)(2,1)S(1)}, u32[]{:S(2)}, u32[]{:S(2)}) collective-permute-start(bf16[1,34,1,320]{3,2,1,0:T(2,128)(2,1)S(1)} %get-tuple-element.27), channel_id=1, source_target_pairs={{1,0},{2,1},{3,2},{5,4},{6,5},{7,6},{9,8},{10,9},{11,10},{13,12},{... | collective-permute-start | bytes 65288 | tf_op jit(solution)/shard_map/ppermute | solution.py:18
  134.0 2.3 %copy-start.4 = (bf16[1024,320]{0,1:T(8,128)(2,1)S(1)}, bf16[1024,320]{0,1:T(8,128)(2,1)}, u32[]{:S(2)}) copy-start(bf16[1024,320]{0,1:T(8,128)(2,1)} %copy.20) | copy-start | bytes 1966084
  136.3 2.9 %copy-start.5 = (bf16[1024,320]{0,1:T(8,128)(2,1)S(1)}, bf16[1024,320]{0,1:T(8,128)(2,1)}, u32[]{:S(2)}) copy-start(bf16[1024,320]{0,1:T(8,128)(2,1)} %copy.22) | copy-start | bytes 1966084
  136.3 3.8 %copy-start.1 = (f32[1024,320]{0,1:T(8,128)S(1)}, f32[1024,320]{0,1:T(8,128)}, u32[]{:S(2)}) copy-start(f32[1024,320]{0,1:T(8,128)} %get-tuple-element.45) | copy-start | bytes 3932164
  140.0 4.8 %copy-start.2 = (bf16[1,32,32,320]{3,2,1,0:T(8,128)(2,1)S(1)}, bf16[1,32,32,320]{3,2,1,0:T(8,128)(2,1)}, u32[]{:S(2)}) copy-start(bf16[1,32,32,320]{3,2,1,0:T(8,128)(2,1)} %get-tuple-element.13) | copy-start | bytes 1966084
  144.9 2.4 %copy-start.6 = (bf16[1024,320]{0,1:T(8,128)(2,1)S(1)}, bf16[1024,320]{0,1:T(8,128)(2,1)}, u32[]{:S(2)}) copy-start(bf16[1024,320]{0,1:T(8,128)(2,1)} %copy.24) | copy-start | bytes 1966084
  144.9 3.3 %copy-start.3 = (bf16[1024,320]{0,1:T(8,128)(2,1)S(1)}, bf16[1024,320]{0,1:T(8,128)(2,1)}, u32[]{:S(2)}) copy-start(bf16[1024,320]{0,1:T(8,128)(2,1)} %copy.25) | copy-start | bytes 1966084
  147.3 2.7 %copy-start.7 = (bf16[320,9,320]{0,2,1:T(8,128)(2,1)S(1)}, bf16[320,9,320]{0,2,1:T(8,128)(2,1)}, u32[]{:S(2)}) copy-start(bf16[320,9,320]{0,2,1:T(8,128)(2,1)} %copy.27) | copy-start | bytes 5529604
  147.3 2.7 %copy-start.8 = (f32[1024,320]{0,1:T(8,128)S(1)}, f32[1024,320]{0,1:T(8,128)}, u32[]{:S(2)}) copy-start(f32[1024,320]{0,1:T(8,128)} %copy.28) | copy-start | bytes 3932164
Sparse Core Ops, SparseCore 0:
  8.9 35.3 all-gather.2
  45.8 34.6 all-gather.4
where the time goes:
time: 164 us; the launch traced here: 163 us
  local copies, waits for them, and re-layouts  47.5 us (29%)
  blocking collectives  44.6 us (27%)
  starting transfers between devices  35.5 us (22%)
  between operations  13.6 us (8%)
  matrix products  11.6 us (7%)
  other arithmetic  8 us (5%)
  waiting for transfers between devices  2.03 us (1%)
    psum x2, blocking collectives, normalize(): lax.psum((jnp.sum(grouped, axis=(1, 3)), jnp.sum(grouped * grouped, axis=...  44.6 us
    ppermute x4, starting transfers between devices, extended(): after = lax.ppermute(initial, axis, down)  23.6 us
    concatenate x10, local copies, waits for them, and re-layouts, tap_stack(): return jnp.concatenate(pieces, axis=-1).reshape(-1, 9 * width)  20.4 us
    ppermute x4, starting transfers between devices, extended(): before = lax.ppermute(last, axis, up)  11.9 us
    dot_general x2, matrix products, finish(): lax.dot_general(stacked, flat_kernel, (((1,), (1,)), ((), ())), preferred...  11.6 us
    unnamed x27, local copies, waits for them, and re-layouts  9.62 us
    all_gather x2, local copies, waits for them, and re-layouts, convolve_gathered(): whole_kernel = lax.all_gather(kernel, 'dp', axis=0, tiled=True)  8.4 us
    slice x3, local copies, waits for them, and re-layouts, tap_stack(): padded[:, shift_row:shift_row + tile_rows, shift_col:shift_col + tile_col...  3.64 us
  transfers between devices with their start and end apart: 10, of which 2 were waited for; matrix products, arithmetic and copies ran while one was open for 24% of the time, Pallas kernels for 0%

commit v1 on v0

--- a/solution.py
+++ b/solution.py
@@ -58,7 +58,9 @@
 
 
 def convolve_gathered(stacked, kernel, skip_flat):
-    whole_kernel = lax.all_gather(kernel, "dp", axis=0, tiled=True)
+    whole_kernel = jnp.concatenate(
+        lax.all_to_all(jnp.stack([kernel] * lax.axis_size("dp")), "dp", 0, 0), axis=0
+    )
     return finish(stacked, whole_kernel, skip_flat)
 
 

time: 164 us -> 183 us (1.12)
  local copies, waits for them, and re-layouts: 47.5 us -> 64.8 us
  between operations: 13.6 us -> 0.28 us
  starting transfers between devices: 35.5 us -> 46 us
  other arithmetic: 8 us -> 13.8 us
  waiting for transfers between devices: 2.03 us -> 0.03 us
    all_to_all x0 -> x2, local copies, waits for them, and re-layouts: none -> 13 us  [convolve_gathered(): lax.all_to_all(jnp.stack([kernel] * lax.axis_size('dp')), 'dp', 0, 0)]
    another operation x0 -> x2, local copies, waits for them, and re-layouts: none -> 10.3 us  [finish(): flat_kernel = whole_kernel.reshape(whole_kernel.shape[0], -1)]
    all_to_all x0 -> x2, starting transfers between devices: none -> 8.7 us  [convolve_gathered(): lax.all_to_all(jnp.stack([kernel] * lax.axis_size('dp')), 'dp', 0, 0)]
    all_gather x2 -> x0, local copies, waits for them, and re-layouts: 8.4 us -> none  [convolve_gathered(): whole_kernel = lax.all_gather(kernel, 'dp', axis=0, tiled=True)]
    another operation x0 -> x2, other arithmetic: none -> 5.22 us  [convolve_gathered(): jnp.stack([kernel] * lax.axis_size('dp'))]
    unnamed x27 -> x29, local copies, waits for them, and re-layouts: 9.62 us -> 9.95 us
  transfers between devices with their start and end apart: 10 -> 10, of which waited for: 2 -> 0; matrix products, arithmetic and copies ran while one was open for 24% -> 32% of each run, Pallas kernels for 0% -> 0%
where the time goes in v1:
time: 183 us; the launch traced here: 181 us
  local copies, waits for them, and re-layouts  64.8 us (35%)
  starting transfers between devices  46 us (25%)
  blocking collectives  44.6 us (24%)
  other arithmetic  13.8 us (8%)
  matrix products  11.6 us (6%)
    psum x2, blocking collectives, normalize(): lax.psum((jnp.sum(grouped, axis=(1, 3)), jnp.sum(grouped * grouped, axis=...  44.6 us
    ppermute x4, starting transfers between devices, extended(): after = lax.ppermute(initial, axis, down)  25 us
    concatenate x10, local copies, waits for them, and re-layouts, tap_stack(): return jnp.concatenate(pieces, axis=-1).reshape(-1, 9 * width)  21.1 us
    all_to_all x2, local copies, waits for them, and re-layouts, convolve_gathered(): lax.all_to_all(jnp.stack([kernel] * lax.axis_size('dp')), 'dp', 0, 0)  13 us
    ppermute x4, starting transfers between devices, extended(): before = lax.ppermute(last, axis, up)  12.3 us
    dot_general x2, matrix products, finish(): lax.dot_general(stacked, flat_kernel, (((1,), (1,)), ((), ())), preferred...  11.6 us
    another operation x2, local copies, waits for them, and re-layouts, finish(): flat_kernel = whole_kernel.reshape(whole_kernel.shape[0], -1)  10.3 us
    unnamed x29, local copies, waits for them, and re-layouts  9.95 us
  transfers between devices with their start and end apart: 10, of which 0 were waited for; matrix products, arithmetic and copies ran while one was open for 32% of the time, Pallas kernels for 0%

profile of v1, /device:TPU:9, one launch (start us, length us, event | category | flops | bytes accessed | tf_op | source)
XLA Modules:
  0.0 181.1 jit_solution(3912073632823896451)
XLA Ops:
  1.9 22.3 %all-reduce.1 = (f32[1,32]{1,0:T(1,128)S(1)}, f32[1,32]{1,0:T(1,128)S(1)}) all-reduce(f32[1,32]{1,0:T(1,128)S(1)} %bitcast.67, f32[1,32]{1,0:T(1,128)S(1)} %bitcast.65), channel_id=1, replica_groups=mesh['dp'=2,'row'=4,'col'=4] {'row','col'}, use_global_device_ids=true, to_apply=%region_5.6 | all-reduce | flops 64 | bytes 512 | tf_op jit(solution)/shard_map/psum | solution.py:28
  26.3 3.2 %collective-permute-start = (bf16[1,1,32,320]{3,2,1,0:T(8,128)(2,1)S(1)}, bf16[1,1,32,320]{3,2,1,0:T(8,128)(2,1)S(1)}, u32[]{:S(2)}, u32[]{:S(2)}) collective-permute-start(bf16[1,1,32,320]{3,2,1,0:T(8,128)(2,1)S(1)} %get-tuple-element.39), channel_id=1, source_target_pairs={{0,4},{4,8},{8,12},{1,5},{5,9},{9,13},{2,6},{6,10},{10,14},{3,7},{... | collective-permute-start | bytes 61448 | tf_op jit(solution)/shard_map/ppermute | solution.py:17
  29.5 7.6 %collective-permute-start.1 = (bf16[1,1,32,320]{3,2,1,0:T(8,128)(2,1)S(1)}, bf16[1,1,32,320]{3,2,1,0:T(8,128)(2,1)S(1)}, u32[]{:S(2)}, u32[]{:S(2)}) collective-permute-start(bf16[1,1,32,320]{3,2,1,0:T(8,128)(2,1)S(1)} %get-tuple-element.40), channel_id=1, source_target_pairs={{4,0},{8,4},{12,8},{5,1},{9,5},{13,9},{6,2},{10,6},{14,10},{7,3},{... | collective-permute-start | bytes 61448 | tf_op jit(solution)/shard_map/ppermute | solution.py:18
  39.0 3.8 %all-to-all-start = ((bf16[2,160,9,320]{3,1,2,0:T(8,128)(2,1)}), bf16[2,160,9,320]{3,1,2,0:T(8,128)(2,1)S(1)}, u32[]{:S(2)}, u32[]{:S(2)}) async-start(bf16[2,160,9,320]{3,1,2,0:T(8,128)(2,1)} %pad_maximum_fusion), calls=%async_computation | async-start | bytes 4423680 | tf_op jit(solution)/shard_map/all_to_all | solution.py:62
  42.8 3.4 %pad_maximum_fusion.1 = bf16[2,160,9,320]{3,1,2,0:T(8,128)(2,1)} fusion(bf16[1,160,9,320]{3,1,2,0:T(8,128)(2,1)} %bitcast.63), kind=kLoop, calls=%fused_computation.1 | loop fusion | flops 921600 | bytes 2764800 | tf_op jit(solution)/shard_map/stack | solution.py:62
  46.3 3.3 %collective-permute-start.2 = (bf16[1,34,1,320]{3,2,1,0:T(2,128)(2,1)S(1)}, bf16[1,34,1,320]{3,2,1,0:T(2,128)(2,1)S(1)}, u32[]{:S(2)}, u32[]{:S(2)}) collective-permute-start(bf16[1,34,1,320]{3,2,1,0:T(2,128)(2,1)S(1)} %get-tuple-element.32), channel_id=1, source_target_pairs={{0,1},{1,2},{2,3},{4,5},{5,6},{6,7},{8,9},{9,10},{10,11},{12,13},{... | collective-permute-start | bytes 65288 | tf_op jit(solution)/shard_map/ppermute | solution.py:17
  49.5 4.6 %collective-permute-start.3 = (bf16[1,34,1,320]{3,2,1,0:T(2,128)(2,1)S(1)}, bf16[1,34,1,320]{3,2,1,0:T(2,128)(2,1)S(1)}, u32[]{:S(2)}, u32[]{:S(2)}) collective-permute-start(bf16[1,34,1,320]{3,2,1,0:T(2,128)(2,1)S(1)} %get-tuple-element.31), channel_id=1, source_target_pairs={{1,0},{2,1},{3,2},{5,4},{6,5},{7,6},{9,8},{10,9},{11,10},{13,12},{... | collective-permute-start | bytes 65288 | tf_op jit(solution)/shard_map/ppermute | solution.py:18
  56.2 2.6 %fusion.6 = (bf16[1,32,32,320]{3,2,1,0:T(8,128)(2,1)}, bf16[1,32,32,320]{3,2,1,0:T(8,128)(2,1)}, bf16[1,32,32,320]{3,2,1,0:T(8,128)(2,1)}, bf16[1,32,32,320]{3,2...) fusion(bf16[1,34,33,320]{3,2,1,0:T(8,128)(2,1)S(1)} %get-tuple-element.29, ...), kind=kLoop, calls=%fused_computation.42 | loop fusion | bytes 7864320 | tf_op jit(solution)/shard_map/slice | solution.py:43
  58.7 10.4 %concatenate.96 = bf16[1024,2880]{1,0:T(8,128)(2,1)} concatenate(bf16[1024,320]{1,0:T(8,128)(2,1)} %bitcast.49, bf16[1024,320]{1,0:T(8,128)(2,1)} %bitcast.54, bf16[1024,320]{1,0:T(8,128)(2,1)} %bitcast.48, bf16[1024,320]{1,0:T(8,128)(2,1)} %bitcast.50, bf16[1024,320]{1,0:T(8,128)(2,1)S(1)} %bitcast.43, bf16[1024,320]{1,0:T(8,128)(2,1)} %bitcast.47, bf16[1024,320]{1,0:T(8,128)(2,1)} %bitcast.51, ...), dimensions={1} | concatenate | bytes 11796480 | tf_op jit(solution)/shard_map/concatenate | solution.py:47
  70.5 4.9 %all-to-all-start.1 = ((bf16[2,160,9,320]{3,1,2,0:T(8,128)(2,1)}), bf16[2,160,9,320]{3,1,2,0:T(8,128)(2,1)}, u32[]{:S(2)}, u32[]{:S(2)}) async-start(bf16[2,160,9,320]{3,1,2,0:T(8,128)(2,1)} %pad_maximum_fusion.1), calls=%async_computation.1 | async-start | bytes 4423680 | tf_op jit(solution)/shard_map/all_to_all | solution.py:62
  75.4 5.9 %copy.17 = bf16[2,160,9,320]{1,0,3,2:T(2,128)(2,1)S(1)} copy(bf16[2,160,9,320]{3,1,2,0:T(8,128)(2,1)} %copy-done) | data formatting | bytes 3686400 | tf_op jit(solution)/shard_map/all_to_all | solution.py:62
  81.4 2.9 %reshape_reshape.6 = bf16[320,2880]{0,1:T(8,128)(2,1)} reshape(bf16[2,160,9,320]{1,0,3,2:T(2,128)(2,1)S(1)} %copy.17) | data formatting | bytes 3686400 | tf_op jit(solution)/shard_map/reshape;reshape | solution.py:51
  84.2 6.7 %fusion.3 = (f32[320]{0:T(512)S(1)}, f32[320]{0:T(512)S(1)}, f32[1024,320]{0,1:T(8,128)}) fusion(bf16[1024,2880]{1,0:T(8,128)(2,1)} %concatenate.96, bf16[320,2880]{0,1:T(8,128)(2,1)} %reshape_reshape.6), kind=kOutput, calls=%fused_computation.39 | convolution fusion | flops 1889074688 | bytes 9054720 | tf_op jit(solution)/shard_map/dot_general | solution.py:52
  91.4 22.3 %all-reduce = (f32[1,32]{1,0:T(1,128)S(1)}, f32[1,32]{1,0:T(1,128)S(1)}) all-reduce(f32[1,32]{1,0:T(1,128)S(1)} %bitcast.66, f32[1,32]{1,0:T(1,128)S(1)} %bitcast.64), channel_id=1, replica_groups=mesh['dp'=2,'row'=4,'col'=4] {'row','col'}, use_global_device_ids=true, to_apply=%region_11.12 | all-reduce | flops 64 | bytes 512 | tf_op jit(solution)/shard_map/psum | solution.py:28
  118.4 8.0 %collective-permute-start.5 = (bf16[1,1,32,320]{3,2,1,0:T(8,128)(2,1)S(1)}, bf16[1,1,32,320]{3,2,1,0:T(8,128)(2,1)S(1)}, u32[]{:S(2)}, u32[]{:S(2)}) collective-permute-start(bf16[1,1,32,320]{3,2,1,0:T(8,128)(2,1)S(1)} %get-tuple-element.36), channel_id=1, source_target_pairs={{4,0},{8,4},{12,8},{5,1},{9,5},{13,9},{6,2},{10,6},{14,10},{7,3},{... | collective-permute-start | bytes 61448 | tf_op jit(solution)/shard_map/ppermute | solution.py:18
  127.8 7.1 %copy.27 = bf16[2,160,9,320]{1,0,3,2:T(2,128)(2,1)} copy(bf16[2,160,9,320]{3,1,2,0:T(8,128)(2,1)} %all-to-all-done.1) | data formatting | bytes 3686400 | tf_op jit(solution)/shard_map/all_to_all | solution.py:62
  134.9 7.4 %reshape_reshape.7 = bf16[320,2880]{0,1:T(8,128)(2,1)} reshape(bf16[2,160,9,320]{1,0,3,2:T(2,128)(2,1)} %copy.27) | data formatting | bytes 3686400 | tf_op jit(solution)/shard_map/reshape;reshape | solution.py:51
  142.4 3.9 %collective-permute-start.6 = (bf16[1,34,1,320]{3,2,1,0:T(2,128)(2,1)S(1)}, bf16[1,34,1,320]{3,2,1,0:T(2,128)(2,1)S(1)}, u32[]{:S(2)}, u32[]{:S(2)}) collective-permute-start(bf16[1,34,1,320]{3,2,1,0:T(2,128)(2,1)S(1)} %get-tuple-element.28), channel_id=1, source_target_pairs={{0,1},{1,2},{2,3},{4,5},{5,6},{6,7},{8,9},{9,10},{10,11},{12,13},{... | collective-permute-start | bytes 65288 | tf_op jit(solution)/shard_map/ppermute | solution.py:17
  146.3 4.8 %collective-permute-start.7 = (bf16[1,34,1,320]{3,2,1,0:T(2,128)(2,1)S(1)}, bf16[1,34,1,320]{3,2,1,0:T(2,128)(2,1)S(1)}, u32[]{:S(2)}, u32[]{:S(2)}) collective-permute-start(bf16[1,34,1,320]{3,2,1,0:T(2,128)(2,1)S(1)} %get-tuple-element.27), channel_id=1, source_target_pairs={{1,0},{2,1},{3,2},{5,4},{6,5},{7,6},{9,8},{10,9},{11,10},{13,12},{... | collective-permute-start | bytes 65288 | tf_op jit(solution)/shard_map/ppermute | solution.py:18
  157.9 2.3 %copy.21 = bf16[1024,320]{0,1:T(8,128)(2,1)} copy(bf16[1024,320]{1,0:T(8,128)(2,1)} %bitcast.59) | data formatting | bytes 1310720 | tf_op jit(solution)/shard_map/concatenate | solution.py:47
  160.2 2.2 %copy.22 = bf16[1024,320]{0,1:T(8,128)(2,1)} copy(bf16[1024,320]{1,0:T(8,128)(2,1)} %bitcast.57) | data formatting | bytes 1310720 | tf_op jit(solution)/shard_map/concatenate | solution.py:47
  163.3 2.0 %constant_dynamic-update-slice_fusion.5 = bf16[1024,2880]{0,1:T(8,128)(2,1)} fusion(bf16[1024,2880]{0,1:T(8,128)(2,1)} %constant_dynamic-update-slice_fusion.6, bf16[1024,320]{0,1:T(8,128)(2,1)} %copy.21), kind=kLoop, calls=%fused_computation.32 | loop fusion | bytes 1310720
  171.1 2.1 %constant_dynamic-update-slice_fusion.2 = bf16[1024,2880]{0,1:T(8,128)(2,1)} fusion(bf16[1024,2880]{0,1:T(8,128)(2,1)} %constant_dynamic-update-slice_fusion.3, bf16[1024,320]{0,1:T(8,128)(2,1)} %copy.24), kind=kLoop, calls=%fused_computation.29 | loop fusion | bytes 1310720
  175.0 4.9 %fusion = bf16[1024,320]{0,1:T(8,128)(2,1)S(1)} fusion(f32[1024,320]{0,1:T(8,128)S(1)} %copy-done.8, bf16[1024,2880]{0,1:T(8,128)(2,1)} %constant_dynamic-update-slice_fusion, bf16[320,2880]{0,1:T(8,128)(2,1)S(1)} %copy-done.7), kind=kOutput, calls=%fused_computation.6 | convolution fusion | flops 1888092160 | bytes 9707520 | tf_op jit(solution)/shard_map/dot_general | solution.py:52
  (81 shorter events, 32.2 us)
Async XLA Ops:
  0.0 37.1 %copy-start.9 = (bf16[160,9,320]{2,0,1:T(8,128)(2,1)S(1)}, bf16[160,9,320]{2,0,1:T(8,128)(2,1)}, u32[]{:S(2)}) copy-start(bf16[160,9,320]{2,0,1:T(8,128)(2,1)} %param.7) | copy-start | bytes 2764804
  26.3 19.8 %collective-permute-start = (bf16[1,1,32,320]{3,2,1,0:T(8,128)(2,1)S(1)}, bf16[1,1,32,320]{3,2,1,0:T(8,128)(2,1)S(1)}, u32[]{:S(2)}, u32[]{:S(2)}) collective-permute-start(bf16[1,1,32,320]{3,2,1,0:T(8,128)(2,1)S(1)} %get-tuple-element.39), channel_id=1, source_target_pairs={{0,4},{4,8},{8,12},{1,5},{5,9},{9,13},{2,6},{6,10},{10,14},{3,7},{... | collective-permute-start | bytes 61448 | tf_op jit(solution)/shard_map/ppermute | solution.py:17
  29.5 16.6 %collective-permute-start.1 = (bf16[1,1,32,320]{3,2,1,0:T(8,128)(2,1)S(1)}, bf16[1,1,32,320]{3,2,1,0:T(8,128)(2,1)S(1)}, u32[]{:S(2)}, u32[]{:S(2)}) collective-permute-start(bf16[1,1,32,320]{3,2,1,0:T(8,128)(2,1)S(1)} %get-tuple-element.40), channel_id=1, source_target_pairs={{4,0},{8,4},{12,8},{5,1},{9,5},{13,9},{6,2},{10,6},{14,10},{7,3},{... | collective-permute-start | bytes 61448 | tf_op jit(solution)/shard_map/ppermute | solution.py:18
  39.0 30.2 %all-to-all-start = ((bf16[2,160,9,320]{3,1,2,0:T(8,128)(2,1)}), bf16[2,160,9,320]{3,1,2,0:T(8,128)(2,1)S(1)}, u32[]{:S(2)}, u32[]{:S(2)}) async-start(bf16[2,160,9,320]{3,1,2,0:T(8,128)(2,1)} %pad_maximum_fusion), calls=%async_computation | async-start | bytes 4423680 | tf_op jit(solution)/shard_map/all_to_all | solution.py:62
  46.3 9.3 %collective-permute-start.2 = (bf16[1,34,1,320]{3,2,1,0:T(2,128)(2,1)S(1)}, bf16[1,34,1,320]{3,2,1,0:T(2,128)(2,1)S(1)}, u32[]{:S(2)}, u32[]{:S(2)}) collective-permute-start(bf16[1,34,1,320]{3,2,1,0:T(2,128)(2,1)S(1)} %get-tuple-element.32), channel_id=1, source_target_pairs={{0,1},{1,2},{2,3},{4,5},{5,6},{6,7},{8,9},{9,10},{10,11},{12,13},{... | collective-permute-start | bytes 65288 | tf_op jit(solution)/shard_map/ppermute | solution.py:17
  49.5 6.0 %collective-permute-start.3 = (bf16[1,34,1,320]{3,2,1,0:T(2,128)(2,1)S(1)}, bf16[1,34,1,320]{3,2,1,0:T(2,128)(2,1)S(1)}, u32[]{:S(2)}, u32[]{:S(2)}) collective-permute-start(bf16[1,34,1,320]{3,2,1,0:T(2,128)(2,1)S(1)} %get-tuple-element.31), channel_id=1, source_target_pairs={{1,0},{2,1},{3,2},{5,4},{6,5},{7,6},{9,8},{10,9},{11,10},{13,12},{... | collective-permute-start | bytes 65288 | tf_op jit(solution)/shard_map/ppermute | solution.py:18
  69.2 1.4 copy-start
  70.5 57.3 %all-to-all-start.1 = ((bf16[2,160,9,320]{3,1,2,0:T(8,128)(2,1)}), bf16[2,160,9,320]{3,1,2,0:T(8,128)(2,1)}, u32[]{:S(2)}, u32[]{:S(2)}) async-start(bf16[2,160,9,320]{3,1,2,0:T(8,128)(2,1)} %pad_maximum_fusion.1), calls=%async_computation.1 | async-start | bytes 4423680 | tf_op jit(solution)/shard_map/all_to_all | solution.py:62
  91.0 25.0 %copy-start.10 = (f32[320]{0:T(512)S(1)}, f32[320]{0:T(512)}, u32[]{:S(2)}) copy-start(f32[320]{0:T(512)} %param.8) | copy-start | bytes 3844
  114.1 12.4 %copy-start.1 = (bf16[1,32,32,320]{3,2,1,0:T(8,128)(2,1)S(1)}, bf16[1,32,32,320]{3,2,1,0:T(8,128)(2,1)}, u32[]{:S(2)}) copy-start(bf16[1,32,32,320]{3,2,1,0:T(8,128)(2,1)} %param.5) | copy-start | bytes 1966084
  116.5 25.8 %collective-permute-start.4 = (bf16[1,1,32,320]{3,2,1,0:T(8,128)(2,1)S(1)}, bf16[1,1,32,320]{3,2,1,0:T(8,128)(2,1)S(1)}, u32[]{:S(2)}, u32[]{:S(2)}) collective-permute-start(bf16[1,1,32,320]{3,2,1,0:T(8,128)(2,1)S(1)} %get-tuple-element.35), channel_id=1, source_target_pairs={{0,4},{4,8},{8,12},{1,5},{5,9},{9,13},{2,6},{6,10},{10,14},{3,7},{... | collective-permute-start | bytes 61448 | tf_op jit(solution)/shard_map/ppermute | solution.py:17
  118.4 23.9 %collective-permute-start.5 = (bf16[1,1,32,320]{3,2,1,0:T(8,128)(2,1)S(1)}, bf16[1,1,32,320]{3,2,1,0:T(8,128)(2,1)S(1)}, u32[]{:S(2)}, u32[]{:S(2)}) collective-permute-start(bf16[1,1,32,320]{3,2,1,0:T(8,128)(2,1)S(1)} %get-tuple-element.36), channel_id=1, source_target_pairs={{4,0},{8,4},{12,8},{5,1},{9,5},{13,9},{6,2},{10,6},{14,10},{7,3},{... | collective-permute-start | bytes 61448 | tf_op jit(solution)/shard_map/ppermute | solution.py:18
  142.4 11.3 %collective-permute-start.6 = (bf16[1,34,1,320]{3,2,1,0:T(2,128)(2,1)S(1)}, bf16[1,34,1,320]{3,2,1,0:T(2,128)(2,1)S(1)}, u32[]{:S(2)}, u32[]{:S(2)}) collective-permute-start(bf16[1,34,1,320]{3,2,1,0:T(2,128)(2,1)S(1)} %get-tuple-element.28), channel_id=1, source_target_pairs={{0,1},{1,2},{2,3},{4,5},{5,6},{6,7},{8,9},{9,10},{10,11},{12,13},{... | collective-permute-start | bytes 65288 | tf_op jit(solution)/shard_map/ppermute | solution.py:17
  146.3 7.4 %collective-permute-start.7 = (bf16[1,34,1,320]{3,2,1,0:T(2,128)(2,1)S(1)}, bf16[1,34,1,320]{3,2,1,0:T(2,128)(2,1)S(1)}, u32[]{:S(2)}, u32[]{:S(2)}) collective-permute-start(bf16[1,34,1,320]{3,2,1,0:T(2,128)(2,1)S(1)} %get-tuple-element.27), channel_id=1, source_target_pairs={{1,0},{2,1},{3,2},{5,4},{6,5},{7,6},{9,8},{10,9},{11,10},{13,12},{... | collective-permute-start | bytes 65288 | tf_op jit(solution)/shard_map/ppermute | solution.py:18
  157.9 4.5 %copy-start.4 = (bf16[1024,320]{0,1:T(8,128)(2,1)S(1)}, bf16[1024,320]{0,1:T(8,128)(2,1)}, u32[]{:S(2)}) copy-start(bf16[1024,320]{0,1:T(8,128)(2,1)} %copy.20) | copy-start | bytes 1966084
  162.4 2.9 %copy-start.6 = (bf16[1024,320]{0,1:T(8,128)(2,1)S(1)}, bf16[1024,320]{0,1:T(8,128)(2,1)}, u32[]{:S(2)}) copy-start(bf16[1024,320]{0,1:T(8,128)(2,1)} %copy.22) | copy-start | bytes 1966084
  162.4 3.8 %copy-start.2 = (f32[1024,320]{0,1:T(8,128)S(1)}, f32[1024,320]{0,1:T(8,128)}, u32[]{:S(2)}) copy-start(f32[1024,320]{0,1:T(8,128)} %get-tuple-element.45) | copy-start | bytes 3932164
  168.7 1.5 copy-start.5
  169.9 3.3 %copy-start.3 = (bf16[1024,320]{0,1:T(8,128)(2,1)S(1)}, bf16[1024,320]{0,1:T(8,128)(2,1)}, u32[]{:S(2)}) copy-start(bf16[1024,320]{0,1:T(8,128)(2,1)} %copy.25) | copy-start | bytes 1966084
  171.1 3.9 %copy-start.7 = (bf16[320,2880]{0,1:T(8,128)(2,1)S(1)}, bf16[320,2880]{0,1:T(8,128)(2,1)}, u32[]{:S(2)}) copy-start(bf16[320,2880]{0,1:T(8,128)(2,1)} %reshape_reshape.7) | copy-start | bytes 5529604
  171.1 3.9 %copy-start.8 = (f32[1024,320]{0,1:T(8,128)S(1)}, f32[1024,320]{0,1:T(8,128)}, u32[]{:S(2)}) copy-start(f32[1024,320]{0,1:T(8,128)} %copy.28) | copy-start | bytes 3932164
